TPU v7x, 256 devices: a whole 4x4x8 slice. The times are simulated.
256 devices in a mesh: tm: 8 (over y, core), strip: 32 (over z, x).
Axes of the slice: x: 4, y: 4, z: 8, core: 2. Of those that a mesh axis runs over, the one named last changes fastest.
Arguments:
- start_state: float32 [16, 256, 128], P(None, 'strip'), may hold values from -20 to 20
- trajectory: float32 [16, 16, 256, 128], P('tm', None, 'strip'), may hold values from -20 to 20
- history: float32 [3, 16, 16, 256, 128], P(None, 'tm', None, 'strip'), may hold values from -6 to 6
- history_length: int32 [16], P('tm'), may hold values from 1 to 3
- timesteps: int32 [16], P('tm'), may hold values from 0 to 999
- step_size: float32 [16], P('tm'), may hold values from 0.05 to 0.2
- mix_table: int32 [16, 16], replicated, may hold values from -64 to 128, as said below
- time_table: float32 [1000, 320], replicated, may hold values from -6 to 6
- conv_in: bfloat16 [9, 320, 16], replicated, may hold values from -0.5 to 0.5
- norm_gain: float32 [320], replicated, may hold values from 0.1 to 1.9
- norm_bias: float32 [320], replicated, may hold values from -3 to 3
- conv_mid: bfloat16 [9, 320, 320], replicated, may hold values from -0.109375 to 0.109375
- conv_out: bfloat16 [16, 320], replicated, may hold values from -0.3125 to 0.3125
Outputs:
- iterate: float32 [16, 16, 256, 128], P('tm', None, 'strip')
- residual: float32 [16, 16, 256, 128], P('tm', None, 'strip')
Inputs may be any that keep to these rules, and one draw needn't show every extreme that they name: mix_table[j, i] is 0 for i > j and lies in 64 to 128 for i = j.
All inputs are finite; a program needn't handle non-finite values.
Results may differ from a plain program's by a relative error of at most 0.001.
Values may be sent and summed in bfloat16 or wider, within the bound.
A program may use at most 128 MiB of HBM per device.

v0:
```python
import functools

import jax
import jax.numpy as jnp
from jax import lax
from jax.experimental import pallas as pl
from jax.experimental.pallas import tpu as pltpu
from jax.sharding import PartitionSpec as P

F32 = jnp.float32
BF16 = jnp.bfloat16
HIGHEST = lax.Precision.HIGHEST
GROUPS = 32
ITERS = 2
EPSILON = 1e-05
UNIT = 1.0 / 256.0
LANES = 128
CHUNK = 32


def silu(v):
    half = 0.5 * v
    return half + half * jnp.tanh(half)


def kernel(
    T,
    S,
    hl_ref,
    ts_ref,
    step_ref,
    mix_ref,
    gain_ref,
    bias_ref,
    start_ref,
    traj_ref,
    hist_ref,
    cin_ref,
    cout_ref,
    table_hbm,
    cmid_hbm,
    iterate_ref,
    residual_ref,
    table,
    wraw,
    wmid,
    win,
    xin,
    xs,
    early,
    hid,
    gaincol,
    biascol,
    embcol,
    ind,
    sums,
    stat,
    stats,
    fsend,
    frecv,
    msend,
    mrecv,
    sbuf,
    state1,
    base2,
    osend,
    orecv,
    local_sem,
    halo_send,
    halo_recv,
    m_send,
    m_recv,
    s_send,
    s_recv,
    a_send,
    a_recv,
    b_send,
    b_recv,
    o_send,
    o_recv,
):
    t = lax.axis_index("tm")
    s = lax.axis_index("strip")
    steps = 2
    CH = cout_ref.shape[1]
    CIN = cout_ref.shape[0]
    rows = T
    total_steps = steps * T
    count = float(CH // GROUPS * rows * S * LANES)

    def to(src, dst, send, recv, tm, strip):
        return pltpu.make_async_remote_copy(
            src_ref=src,
            dst_ref=dst,
            send_sem=send,
            recv_sem=recv,
            device_id=(tm, strip),
            device_id_type=pl.DeviceIdType.MESH,
        )

    def wait_bytes(ref, sem):
        pltpu.make_async_copy(ref, ref, sem).wait()

    get_table = pltpu.make_async_copy(table_hbm, table, local_sem.at[0])
    get_mid = pltpu.make_async_copy(cmid_hbm, wraw, local_sem.at[1])
    get_table.start()
    get_mid.start()

    for j in range(steps):
        for h in range(rows):
            xin[0, 2 + h, j] = traj_ref[pl.ds(j * CIN * rows + h, CIN, stride=rows), :].astype(BF16)
    send_down = to(xin.at[0, pl.ds(rows, 2)], xin.at[0, pl.ds(0, 2)], halo_send.at[0], halo_recv.at[0], t, s + 1)
    send_up = to(xin.at[0, pl.ds(2, 2)], xin.at[0, pl.ds(rows + 2, 2)], halo_send.at[1], halo_recv.at[1], t, s - 1)

    @pl.when(s < S - 1)
    def _():
        send_down.start()

    @pl.when(s > 0)
    def _():
        send_up.start()

    @pl.when(s == 0)
    def _():
        xin[0, 0:2] = jnp.zeros((2, steps, CIN, LANES), BF16)
        xin[1, 0:2] = jnp.zeros((2, steps, CIN, LANES), BF16)

    @pl.when(s == S - 1)
    def _():
        xin[0, rows + 2 : rows + 4] = jnp.zeros((2, steps, CIN, LANES), BF16)
        xin[1, rows + 2 : rows + 4] = jnp.zeros((2, steps, CIN, LANES), BF16)

    for j in range(steps):
        length = jnp.full((CIN, LANES), hl_ref[j], jnp.int32)
        share = 1.0 / length.astype(F32)
        live = [jnp.where(length > m, share, 0.0) for m in range(3)]
        for h in range(rows):
            own = traj_ref[pl.ds(j * CIN * rows + h, CIN, stride=rows), :]
            past = [
                hist_ref[pl.ds((m * steps + j) * CIN * rows + h, CIN, stride=rows), :] for m in range(3)
            ]
            msend[h, j, 0:CIN] = own + (live[0] * past[0] + live[1] * past[1] + live[2] * past[2])
            msend[h, j, CIN : 2 * CIN] = live[1] * past[0] + live[2] * past[1] - live[0] * own
            msend[h, j, 2 * CIN : 2 * CIN + 8] = live[0][0:8]
    mrecv[t] = msend[t]

    def send_m(k, _):
        other = lax.rem(t + k, T)
        to(msend.at[other], mrecv.at[t], m_send, m_recv, other, s).start()
        return 0

    lax.fori_loop(1, T, send_m, 0)

    row_id = lax.broadcasted_iota(jnp.int32, (CH, CH), 0)
    col_id = lax.broadcasted_iota(jnp.int32, (CH, CH), 1)
    diagonal = row_id == col_id
    gaincol[...] = jnp.sum(
        jnp.where(diagonal, jnp.broadcast_to(gain_ref[...], (CH, CH)), 0.0), axis=1, keepdims=True
    )
    biascol[...] = jnp.sum(
        jnp.where(diagonal, jnp.broadcast_to(bias_ref[...], (CH, CH)), 0.0), axis=1, keepdims=True
    )
    turned = lax.dot_general(
        diagonal.astype(F32).astype(BF16),
        cin_ref[...],
        (((1,), (1,)), ((), ())),
        preferred_element_type=F32,
    )
    win[...] = turned.astype(BF16)
    members = CH // GROUPS
    first = lax.broadcasted_iota(jnp.int32, (2 * CH, LANES), 1) * members
    channel = lax.broadcasted_iota(jnp.int32, (2 * CH, LANES), 0)
    ind[...] = jnp.where((channel >= first) & (channel < first + members), 1.0, 0.0)
    get_table.wait()
    at = lax.broadcasted_iota(jnp.int32, table.shape, 1)
    for j in range(steps):
        embcol[j] = jnp.sum(jnp.where(at == ts_ref[j], table[...], 0.0), axis=1, keepdims=True)

    get_mid.wait()
    low = lax.broadcasted_iota(jnp.int32, (CH, LANES), 1) < 64
    for a in range(3):
        wmid[a, :, 0:256] = wraw[3 * a, :, 0:256]
        wmid[a, :, 640:960] = wraw[3 * a + 2]
        middle = [wraw[3 * a + 1, :, k * LANES : (k + 1) * LANES].astype(F32) for k in range(2)]
        tail = wraw[3 * a + 1, :, 256:320].astype(F32)
        middle.append(jnp.concatenate([tail, tail], axis=1))
        turned_by = [pltpu.roll(m, 64, 1) for m in middle[:2]] + [middle[2]]
        head = wraw[3 * a, :, 256:320].astype(F32)
        before = jnp.concatenate([head, head], axis=1)
        for k in range(3):
            wmid[a, :, 256 + k * LANES : 256 + (k + 1) * LANES] = jnp.where(
                low, before, turned_by[k]
            ).astype(BF16)
            before = turned_by[k]

    @pl.when(s < S - 1)
    def _():
        send_down.wait_send()

    @pl.when(s > 0)
    def _():
        send_up.wait_send()

    @pl.when(s > 0)
    def _():
        send_down.wait_recv()

    @pl.when(s < S - 1)
    def _():
        send_up.wait_recv()

    lane = lax.broadcasted_iota(jnp.int32, (CIN, LANES), 1)
    wide = lax.broadcasted_iota(jnp.int32, (CHUNK, LANES), 1)

    def shifted(x, lanes):
        left = jnp.where(lanes == 0, 0.0, pltpu.roll(x, 1, 1))
        right = jnp.where(lanes == LANES - 1, 0.0, pltpu.roll(x, LANES - 1, 1))
        return left, right

    def first_conv(it, j):
        for r in range(rows + 4):
            block = xin[it, r, j]
            left, right = shifted(block.astype(F32), lane)
            xs[0:CIN, r * LANES : (r + 1) * LANES] = left.astype(BF16)
            xs[CIN : 2 * CIN, r * LANES : (r + 1) * LANES] = block
            xs[2 * CIN : 3 * CIN, r * LANES : (r + 1) * LANES] = right.astype(BF16)
        for r in range(0, rows + 2, 2):
            taps = jnp.concatenate(
                [xs[:, (r + a) * LANES : (r + a + 2) * LANES] for a in range(3)], axis=0
            )
            early[j, :, r * LANES : (r + 2) * LANES] = (
                jnp.dot(win[...], taps, preferred_element_type=F32) + embcol[j]
            )

    def send_sums(it, j):
        k = it * steps + j

        def add_up(c, _):
            at = pl.multiple_of(c * CHUNK, CHUNK)
            total = jnp.zeros((CHUNK, LANES), F32)
            square = jnp.zeros((CHUNK, LANES), F32)
            for r in range(1, rows + 1):
                x = early[j, pl.ds(at, CHUNK), r * LANES : (r + 1) * LANES]
                total += x
                square += x * x
            sums[pl.ds(at, CHUNK)] = total
            sums[pl.ds(CH + at, CHUNK)] = square
            return 0

        lax.fori_loop(0, CH // CHUNK, add_up, 0)
        by_channel = lax.dot_general(
            jnp.ones((8, LANES), F32), sums[...], (((1,), (1,)), ((), ())), precision=HIGHEST,
            preferred_element_type=F32,
        )
        by_group = jnp.dot(by_channel, ind[...], precision=HIGHEST, preferred_element_type=F32)
        stat[k] = by_group[0:1]
        stats[k, s] = by_group[0:1]

        def send(i, _):
            other = lax.rem(s + i, S)
            to(stat.at[k], stats.at[k, s], s_send.at[k], s_recv.at[k], t, other).start()
            return 0

        lax.fori_loop(1, S, send, 0)

    def normalise(it, j):
        k = it * steps + j
        wait_bytes(stats.at[k, pl.ds(0, S - 1)], s_send.at[k])
        wait_bytes(stats.at[k, pl.ds(0, S - 1)], s_recv.at[k])
        total = jnp.sum(stats[k], axis=0) * (1.0 / count)
        total = jnp.broadcast_to(total, (8, LANES))
        variance = jnp.maximum(pltpu.roll(total, LANES - GROUPS, 1) - total * total, 0.0)
        scale = 1.0 / jnp.sqrt(variance + EPSILON)
        mean_row, scale_row = total[0:1], scale[0:1]

        def body(c, _):
            at = pl.multiple_of(c * CHUNK, CHUNK)
            which = ind[pl.ds(at, CHUNK)]
            mean = jnp.sum(jnp.where(which > 0.5, mean_row, 0.0), axis=1, keepdims=True)
            factor = jnp.sum(jnp.where(which > 0.5, scale_row, 0.0), axis=1, keepdims=True)
            factor = factor * gaincol[pl.ds(at, CHUNK)]
            offset = biascol[pl.ds(at, CHUNK)]
            for r in range(rows + 2):
                x = early[j, pl.ds(at, CHUNK), r * LANES : (r + 1) * LANES]
                x = silu((x - mean) * factor + offset)
                if r == 0:
                    x = jnp.where(s > 0, x, 0.0)
                if r == rows + 1:
                    x = jnp.where(s < S - 1, x, 0.0)
                left, right = shifted(x, wide)
                cells = slice(r * LANES, (r + 1) * LANES)
                hid[j, pl.ds(at, CHUNK), cells] = left.astype(BF16)
                hid[j, pl.ds(CH + at, CHUNK), cells] = x.astype(BF16)
                hid[j, pl.ds(2 * CH + at, CHUNK), cells] = right.astype(BF16)
            return 0

        lax.fori_loop(0, CH // CHUNK, body, 0)

    def second_conv(it, j):
        for p in range(rows // 2):
            late = None
            for a in range(3):
                product = jnp.dot(
                    wmid[a],
                    hid[j, :, (2 * p + a) * LANES : (2 * p + a + 2) * LANES],
                    preferred_element_type=F32,
                )
                late = product if late is None else late + product
            active = silu(late).astype(BF16)
            field = jnp.dot(cout_ref[...], active, preferred_element_type=F32)
            drift = field * step_ref[j]
            for h in range(2):
                row = 2 * p + h
                fsend[it, row, j] = drift[:, h * LANES : (h + 1) * LANES]

                @pl.when(t == row)
                def _():
                    frecv[it, row, j] = drift[:, h * LANES : (h + 1) * LANES]

                @pl.when(t != row)
                def _():
                    to(fsend.at[it, row, j], frecv.at[it, t, j], a_send.at[it], a_recv.at[it], row, s).start()

    def row_guess(it):
        wait_bytes(frecv.at[it, pl.ds(0, T - 1)], a_send.at[it])
        wait_bytes(frecv.at[it, pl.ds(0, T - 1)], a_recv.at[it])
        guess = [start_ref[pl.ds(t, CIN, stride=rows), :]]
        for i in range(total_steps - 1):
            guess.append(guess[-1] + frecv[it, i // steps, i % steps])
        return guess

    def mixed(guess, anchor, j):
        total = guess[j]
        for i in range(j + 1):
            total = total + (mix_ref[j, i].astype(F32) * UNIT) * anchor[i]
        return total

    for it in range(ITERS):
        for j in range(steps):
            first_conv(it, j)
            send_sums(it, j)
        for j in range(steps):
            normalise(it, j)
            second_conv(it, j)
        if it == 0:
            wait_bytes(mrecv.at[pl.ds(0, T - 1)], m_send)
            wait_bytes(mrecv.at[pl.ds(0, T - 1)], m_recv)
            guess = row_guess(it)
            anchor = [
                guess[i] - mrecv[i // steps, i % steps, 0:CIN] for i in range(total_steps)
            ]
            for j in range(total_steps):
                new = mixed(guess, anchor, j)
                sbuf[j] = new.astype(BF16)
                state1[j] = new
                share = mrecv[j // steps, j % steps, 2 * CIN : 2 * CIN + 8]
                share = jnp.concatenate([share, share], axis=0)
                base2[j] = new + (share * guess[j] + mrecv[j // steps, j % steps, CIN : 2 * CIN])
            xin[1, 2 + t] = sbuf[pl.ds(steps * t, steps)]

            def send_row(k, _):
                other = lax.rem(t + k, T)
                to(sbuf.at[pl.ds(steps * other, steps)], xin.at[1, 2 + t], b_send.at[0], b_recv.at[0], other, s).start()
                return 0

            lax.fori_loop(1, T, send_row, 0)

            below = (t >= rows - 2) & (s < S - 1)
            above = (t < 2) & (s > 0)

            @pl.when(below)
            def _():
                def send_below(k, _):
                    to(sbuf.at[pl.ds(steps * k, steps)], xin.at[1, t - (rows - 2)], b_send.at[1], b_recv.at[1], k, s + 1).start()
                    return 0

                lax.fori_loop(0, T, send_below, 0)

            @pl.when(above)
            def _():
                def send_above(k, _):
                    to(sbuf.at[pl.ds(steps * k, steps)], xin.at[1, rows + 2 + t], b_send.at[2], b_recv.at[2], k, s - 1).start()
                    return 0

                lax.fori_loop(0, T, send_above, 0)

            wait_bytes(sbuf.at[pl.ds(0, steps * (T - 1))], b_send.at[0])

            @pl.when(below)
            def _():
                wait_bytes(sbuf, b_send.at[1])

            @pl.when(above)
            def _():
                wait_bytes(sbuf, b_send.at[2])

            wait_bytes(sbuf.at[pl.ds(0, steps * (T - 1))], b_recv.at[0])

            @pl.when(s > 0)
            def _():
                wait_bytes(sbuf.at[pl.ds(0, steps * 2)], b_recv.at[1])

            @pl.when(s < S - 1)
            def _():
                wait_bytes(sbuf.at[pl.ds(0, steps * 2)], b_recv.at[2])

        else:
            guess = row_guess(it)
            anchor = [guess[i] - base2[i] for i in range(total_steps)]
            for j in range(total_steps):
                osend[j, 1] = guess[j] - state1[j]
                osend[j, 0] = mixed(guess, anchor, j)
            orecv[t] = osend[pl.ds(steps * t, steps)]

            def send_out(k, _):
                other = lax.rem(t + k, T)
                to(osend.at[pl.ds(steps * other, steps)], orecv.at[t], o_send, o_recv, other, s).start()
                return 0

            lax.fori_loop(1, T, send_out, 0)
            wait_bytes(orecv.at[pl.ds(0, T - 1)], o_send)
            wait_bytes(orecv.at[pl.ds(0, T - 1)], o_recv)
            for j in range(steps):
                for h in range(rows):
                    iterate_ref[pl.ds(j * CIN * rows + h, CIN, stride=rows), :] = orecv[h, j, 0]
                    residual_ref[pl.ds(j * CIN * rows + h, CIN, stride=rows), :] = orecv[h, j, 1]


def solution(mesh):
    T = mesh.shape["tm"]
    S = mesh.shape["strip"]

    def shards(
        start_state,
        trajectory,
        history,
        history_length,
        timesteps,
        step_size,
        mix_table,
        time_table,
        conv_in,
        norm_gain,
        norm_bias,
        conv_mid,
        conv_out,
    ):
        steps, CIN, rows, width = trajectory.shape
        CH = conv_out.shape[1]
        total = steps * T
        flat = steps * CIN * rows
        smem = pl.BlockSpec(memory_space=pltpu.SMEM)
        vmem = pl.BlockSpec(memory_space=pltpu.VMEM)
        hbm = pl.BlockSpec(memory_space=pl.ANY)
        dma = pltpu.SemaphoreType.DMA
        iterate, residual = pl.pallas_call(
            functools.partial(kernel, T, S),
            out_shape=(jax.ShapeDtypeStruct((flat, width), F32),) * 2,
            in_specs=[smem] * 4 + [vmem] * 7 + [hbm] * 2,
            out_specs=(vmem, vmem),
            scratch_shapes=[
                pltpu.VMEM((CH, time_table.shape[0]), F32),
                pltpu.VMEM((9, CH, CH), BF16),
                pltpu.VMEM((3, CH, 3 * CH), BF16),
                pltpu.VMEM((CH, 9 * CIN), BF16),
                pltpu.VMEM((ITERS, rows + 4, steps, CIN, width), BF16),
                pltpu.VMEM((3 * CIN, (rows + 4) * width), BF16),
                pltpu.VMEM((steps, CH, (rows + 2) * width), F32),
                pltpu.VMEM((steps, 3 * CH, (rows + 2) * width), BF16),
                pltpu.VMEM((CH, 1), F32),
                pltpu.VMEM((CH, 1), F32),
                pltpu.VMEM((steps, CH, 1), F32),
                pltpu.VMEM((2 * CH, width), F32),
                pltpu.VMEM((2 * CH, width), F32),
                pltpu.VMEM((ITERS * steps, 1, width), F32),
                pltpu.VMEM((ITERS * steps, S, 1, width), F32),
                pltpu.VMEM((ITERS, rows, steps, CIN, width), F32),
                pltpu.VMEM((ITERS, T, steps, CIN, width), F32),
                pltpu.VMEM((rows, steps, 2 * CIN + 8, width), F32),
                pltpu.VMEM((T, steps, 2 * CIN + 8, width), F32),
                pltpu.VMEM((total, CIN, width), BF16),
                pltpu.VMEM((total, CIN, width), F32),
                pltpu.VMEM((total, CIN, width), F32),
                pltpu.VMEM((total, 2, CIN, width), F32),
                pltpu.VMEM((rows, steps, 2, CIN, width), F32),
                dma((2,)),
                dma((2,)),
                dma((2,)),
                dma,
                dma,
                dma((ITERS * steps,)),
                dma((ITERS * steps,)),
                dma((ITERS,)),
                dma((ITERS,)),
                dma((3,)),
                dma((3,)),
                dma,
                dma,
            ],
            compiler_params=pltpu.CompilerParams(
                has_side_effects=True, vmem_limit_bytes=56 * 1024 * 1024
            ),
        )(
            history_length,
            timesteps,
            step_size,
            mix_table,
            norm_gain.reshape(1, CH),
            norm_bias.reshape(1, CH),
            start_state.reshape(CIN * rows, width),
            trajectory.reshape(flat, width),
            history.reshape(history.shape[0] * flat, width),
            jnp.swapaxes(conv_in, 1, 2).reshape(9 * CIN, CH),
            conv_out,
            time_table.T,
            conv_mid,
        )
        return (
            iterate.reshape(trajectory.shape),
            residual.reshape(trajectory.shape),
        )

    return jax.shard_map(
        shards,
        mesh=mesh,
        in_specs=(
            P(None, "strip", None),
            P("tm", None, "strip", None),
            P(None, "tm", None, "strip", None),
            P("tm"),
            P("tm"),
            P("tm"),
            P(),
            P(),
            P(),
            P(),
            P(),
            P(),
            P(),
        ),
        out_specs=(P("tm", None, "strip", None), P("tm", None, "strip", None)),
        check_vma=False,
    )
```

profile of v0, /device:TPU:1, one launch (start us, length us, event | category | flops | bytes accessed | tf_op | source)
XLA Modules:
  0.0 95.7 jit_solution(17519000075787935650)
XLA Ops:
  0.6 1.2 %reshape.28.gain_ref = f32[1,320]{1,0:T(1,128)} reshape(f32[320]{0:T(512)} %param.22) | data formatting | bytes 2560 | tf_op jit(solution)/shard_map/reshape | solution.py:508
  1.9 1.2 %reshape.29.bias_ref = f32[1,320]{1,0:T(1,128)} reshape(f32[320]{0:T(512)} %param.23) | data formatting | bytes 2560 | tf_op jit(solution)/shard_map/reshape | solution.py:509
  3.1 89.4 %shard_map.140 = (f32[256,128]{1,0:T(8,128)}, f32[256,128]{1,0:T(8,128)}) custom-call(s32[2]{0:T(128)} %hl_ref.1, s32[2]{0:T(128)} %ts_ref.1, f32[2]{0:T(128)} %step_ref.1, s32[16,16]{1,0:T(8,128)} %mix_ref.1, f32[1,320]{1,0:T(1,128)} %reshape.28.gain_ref, f32[1,320]{1,0:T(1,128)} %reshape.29.bias_ref, f32[128,128]{1,0:T(8,128)} %bitcast.15, ...), custom_call_target="tpu_custom_call" | custom-call | tf_op jit(solution)/shard_map/pallas_call | solution.py:456
  92.6 1.6 %copy.17 = f32[2,16,8,128]{3,2,1,0:T(8,128)} copy(f32[2,16,8,128]{3,2,1,0:T(8,128)} %bitcast.13) | data formatting | bytes 262144
  94.1 1.6 %copy.18 = f32[2,16,8,128]{3,2,1,0:T(8,128)} copy(f32[2,16,8,128]{3,2,1,0:T(8,128)} %bitcast.12) | data formatting | bytes 262144
where the time goes:
time: 95.9 us; the launch traced here: 95.7 us
  Pallas kernels  89.4 us (93%)
  local copies, waits for them, and re-layouts  5.63 us (6%)
    pallas_call x1, Pallas kernels, shards(): pl.pallas_call(functools.partial(kernel, T, S), out_shape=(jax.ShapeDtype...  89.4 us
    unnamed x2, local copies, waits for them, and re-layouts  3.14 us

commit v1 on v0

--- a/solution.py
+++ b/solution.py
@@ -34,13 +34,14 @@
     bias_ref,
     start_ref,
     traj_ref,
-    hist_ref,
     cin_ref,
     cout_ref,
     table_hbm,
     cmid_hbm,
+    hist_hbm,
     iterate_ref,
     residual_ref,
+    hist_ref,
     table,
     wraw,
     wmid,
@@ -101,6 +102,36 @@
     def wait_bytes(ref, sem):
         pltpu.make_async_copy(ref, ref, sem).wait()
 
+    barrier = pltpu.get_barrier_semaphore()
+
+    def greet(tm, strip):
+        pl.semaphore_signal(
+            barrier, inc=1, device_id=(tm, strip), device_id_type=pl.DeviceIdType.MESH
+        )
+
+    for r in range(2):
+
+        @pl.when(t != rows - 2 + r)
+        def _():
+            greet(rows - 2 + r, lax.rem(s + S - 1, S))
+
+        @pl.when(t != r)
+        def _():
+            greet(r, lax.rem(s + 1, S))
+
+    def greet_column(k, _):
+        greet(lax.rem(t + k, T), s)
+        return 0
+
+    lax.fori_loop(1, T, greet_column, 0)
+
+    def greet_strips(k, _):
+        greet(t, lax.rem(s + k, S))
+        return 0
+
+    lax.fori_loop(1, S, greet_strips, 0)
+    get_past = pltpu.make_async_copy(hist_hbm, hist_ref, local_sem.at[2])
+    get_past.start()
     get_table = pltpu.make_async_copy(table_hbm, table, local_sem.at[0])
     get_mid = pltpu.make_async_copy(cmid_hbm, wraw, local_sem.at[1])
     get_table.start()
@@ -112,14 +143,6 @@
     send_down = to(xin.at[0, pl.ds(rows, 2)], xin.at[0, pl.ds(0, 2)], halo_send.at[0], halo_recv.at[0], t, s + 1)
     send_up = to(xin.at[0, pl.ds(2, 2)], xin.at[0, pl.ds(rows + 2, 2)], halo_send.at[1], halo_recv.at[1], t, s - 1)
 
-    @pl.when(s < S - 1)
-    def _():
-        send_down.start()
-
-    @pl.when(s > 0)
-    def _():
-        send_up.start()
-
     @pl.when(s == 0)
     def _():
         xin[0, 0:2] = jnp.zeros((2, steps, CIN, LANES), BF16)
@@ -129,6 +152,8 @@
     def _():
         xin[0, rows + 2 : rows + 4] = jnp.zeros((2, steps, CIN, LANES), BF16)
         xin[1, rows + 2 : rows + 4] = jnp.zeros((2, steps, CIN, LANES), BF16)
+
+    get_past.wait()
 
     for j in range(steps):
         length = jnp.full((CIN, LANES), hl_ref[j], jnp.int32)
@@ -144,21 +169,14 @@
             msend[h, j, 2 * CIN : 2 * CIN + 8] = live[0][0:8]
     mrecv[t] = msend[t]
 
-    def send_m(k, _):
-        other = lax.rem(t + k, T)
-        to(msend.at[other], mrecv.at[t], m_send, m_recv, other, s).start()
-        return 0
-
-    lax.fori_loop(1, T, send_m, 0)
-
     row_id = lax.broadcasted_iota(jnp.int32, (CH, CH), 0)
     col_id = lax.broadcasted_iota(jnp.int32, (CH, CH), 1)
     diagonal = row_id == col_id
     gaincol[...] = jnp.sum(
-        jnp.where(diagonal, jnp.broadcast_to(gain_ref[...], (CH, CH)), 0.0), axis=1, keepdims=True
+        jnp.where(diagonal, jnp.broadcast_to(gain_ref[...].reshape(1, CH), (CH, CH)), 0.0), axis=1, keepdims=True
     )
     biascol[...] = jnp.sum(
-        jnp.where(diagonal, jnp.broadcast_to(bias_ref[...], (CH, CH)), 0.0), axis=1, keepdims=True
+        jnp.where(diagonal, jnp.broadcast_to(bias_ref[...].reshape(1, CH), (CH, CH)), 0.0), axis=1, keepdims=True
     )
     turned = lax.dot_general(
         diagonal.astype(F32).astype(BF16),
@@ -171,6 +189,31 @@
     first = lax.broadcasted_iota(jnp.int32, (2 * CH, LANES), 1) * members
     channel = lax.broadcasted_iota(jnp.int32, (2 * CH, LANES), 0)
     ind[...] = jnp.where((channel >= first) & (channel < first + members), 1.0, 0.0)
+    edge = (t < 2) | (t >= rows - 2)
+
+    @pl.when(edge)
+    def _():
+        pl.semaphore_wait(barrier, S - 1 + 2 * (T - 1))
+
+    @pl.when(jnp.logical_not(edge))
+    def _():
+        pl.semaphore_wait(barrier, S - 1 + T - 1)
+
+    @pl.when(s < S - 1)
+    def _():
+        send_down.start()
+
+    @pl.when(s > 0)
+    def _():
+        send_up.start()
+
+    def send_m(k, _):
+        other = lax.rem(t + k, T)
+        to(msend.at[other], mrecv.at[t], m_send, m_recv, other, s).start()
+        return 0
+
+    lax.fori_loop(1, T, send_m, 0)
+
     get_table.wait()
     at = lax.broadcasted_iota(jnp.int32, table.shape, 1)
     for j in range(steps):
@@ -235,8 +278,8 @@
     def send_sums(it, j):
         k = it * steps + j
 
-        def add_up(c, _):
-            at = pl.multiple_of(c * CHUNK, CHUNK)
+        def add_up(c):
+            at = c * CHUNK
             total = jnp.zeros((CHUNK, LANES), F32)
             square = jnp.zeros((CHUNK, LANES), F32)
             for r in range(1, rows + 1):
@@ -245,9 +288,9 @@
                 square += x * x
             sums[pl.ds(at, CHUNK)] = total
             sums[pl.ds(CH + at, CHUNK)] = square
-            return 0
-
-        lax.fori_loop(0, CH // CHUNK, add_up, 0)
+
+        for c in range(CH // CHUNK):
+            add_up(c)
         by_channel = lax.dot_general(
             jnp.ones((8, LANES), F32), sums[...], (((1,), (1,)), ((), ())), precision=HIGHEST,
             preferred_element_type=F32,
@@ -273,8 +316,8 @@
         scale = 1.0 / jnp.sqrt(variance + EPSILON)
         mean_row, scale_row = total[0:1], scale[0:1]
 
-        def body(c, _):
-            at = pl.multiple_of(c * CHUNK, CHUNK)
+        def body(c):
+            at = c * CHUNK
             which = ind[pl.ds(at, CHUNK)]
             mean = jnp.sum(jnp.where(which > 0.5, mean_row, 0.0), axis=1, keepdims=True)
             factor = jnp.sum(jnp.where(which > 0.5, scale_row, 0.0), axis=1, keepdims=True)
@@ -292,34 +335,30 @@
                 hid[j, pl.ds(at, CHUNK), cells] = left.astype(BF16)
                 hid[j, pl.ds(CH + at, CHUNK), cells] = x.astype(BF16)
                 hid[j, pl.ds(2 * CH + at, CHUNK), cells] = right.astype(BF16)
+
+        for c in range(CH // CHUNK):
+            body(c)
+
+    def second_conv(it, j):
+        late = None
+        for a in range(3):
+            product = jnp.dot(
+                wmid[a], hid[j, :, a * LANES : (a + rows) * LANES], preferred_element_type=F32
+            )
+            late = product if late is None else late + product
+        active = silu(late).astype(BF16)
+        field = jnp.dot(cout_ref[...], active, preferred_element_type=F32)
+        drift = field * step_ref[j]
+        for h in range(rows):
+            fsend[it, h, j] = drift[:, h * LANES : (h + 1) * LANES]
+
+        def send(k, _):
+            other = lax.rem(t + k, T)
+            to(fsend.at[it, other, j], frecv.at[it, t, j], a_send.at[it], a_recv.at[it], other, s).start()
             return 0
 
-        lax.fori_loop(0, CH // CHUNK, body, 0)
-
-    def second_conv(it, j):
-        for p in range(rows // 2):
-            late = None
-            for a in range(3):
-                product = jnp.dot(
-                    wmid[a],
-                    hid[j, :, (2 * p + a) * LANES : (2 * p + a + 2) * LANES],
-                    preferred_element_type=F32,
-                )
-                late = product if late is None else late + product
-            active = silu(late).astype(BF16)
-            field = jnp.dot(cout_ref[...], active, preferred_element_type=F32)
-            drift = field * step_ref[j]
-            for h in range(2):
-                row = 2 * p + h
-                fsend[it, row, j] = drift[:, h * LANES : (h + 1) * LANES]
-
-                @pl.when(t == row)
-                def _():
-                    frecv[it, row, j] = drift[:, h * LANES : (h + 1) * LANES]
-
-                @pl.when(t != row)
-                def _():
-                    to(fsend.at[it, row, j], frecv.at[it, t, j], a_send.at[it], a_recv.at[it], row, s).start()
+        lax.fori_loop(1, T, send, 0)
+        frecv[it, t, j] = fsend[it, t, j]
 
     def row_guess(it):
         wait_bytes(frecv.at[it, pl.ds(0, T - 1)], a_send.at[it])
@@ -358,13 +397,6 @@
                 base2[j] = new + (share * guess[j] + mrecv[j // steps, j % steps, CIN : 2 * CIN])
             xin[1, 2 + t] = sbuf[pl.ds(steps * t, steps)]
 
-            def send_row(k, _):
-                other = lax.rem(t + k, T)
-                to(sbuf.at[pl.ds(steps * other, steps)], xin.at[1, 2 + t], b_send.at[0], b_recv.at[0], other, s).start()
-                return 0
-
-            lax.fori_loop(1, T, send_row, 0)
-
             below = (t >= rows - 2) & (s < S - 1)
             above = (t < 2) & (s > 0)
 
@@ -384,6 +416,12 @@
 
                 lax.fori_loop(0, T, send_above, 0)
 
+            def send_row(k, _):
+                other = lax.rem(t + k, T)
+                to(sbuf.at[pl.ds(steps * other, steps)], xin.at[1, 2 + t], b_send.at[0], b_recv.at[0], other, s).start()
+                return 0
+
+            lax.fori_loop(1, T, send_row, 0)
             wait_bytes(sbuf.at[pl.ds(0, steps * (T - 1))], b_send.at[0])
 
             @pl.when(below)
@@ -456,9 +494,10 @@
         iterate, residual = pl.pallas_call(
             functools.partial(kernel, T, S),
             out_shape=(jax.ShapeDtypeStruct((flat, width), F32),) * 2,
-            in_specs=[smem] * 4 + [vmem] * 7 + [hbm] * 2,
+            in_specs=[smem] * 4 + [vmem] * 6 + [hbm] * 3,
             out_specs=(vmem, vmem),
             scratch_shapes=[
+                pltpu.VMEM((history.shape[0] * flat, width), F32),
                 pltpu.VMEM((CH, time_table.shape[0]), F32),
                 pltpu.VMEM((9, CH, CH), BF16),
                 pltpu.VMEM((3, CH, 3 * CH), BF16),
@@ -483,7 +522,7 @@
                 pltpu.VMEM((total, CIN, width), F32),
                 pltpu.VMEM((total, 2, CIN, width), F32),
                 pltpu.VMEM((rows, steps, 2, CIN, width), F32),
-                dma((2,)),
+                dma((3,)),
                 dma((2,)),
                 dma((2,)),
                 dma,
@@ -498,22 +537,22 @@
                 dma,
             ],
             compiler_params=pltpu.CompilerParams(
-                has_side_effects=True, vmem_limit_bytes=56 * 1024 * 1024
+                collective_id=0, has_side_effects=True, vmem_limit_bytes=56 * 1024 * 1024
             ),
         )(
             history_length,
             timesteps,
             step_size,
             mix_table,
-            norm_gain.reshape(1, CH),
-            norm_bias.reshape(1, CH),
+            norm_gain,
+            norm_bias,
             start_state.reshape(CIN * rows, width),
             trajectory.reshape(flat, width),
-            history.reshape(history.shape[0] * flat, width),
             jnp.swapaxes(conv_in, 1, 2).reshape(9 * CIN, CH),
             conv_out,
             time_table.T,
             conv_mid,
+            history.reshape(history.shape[0] * flat, width),
         )
         return (
             iterate.reshape(trajectory.shape),

time: 95.9 us -> 68.2 us (0.71)
  Pallas kernels: 89.4 us -> 64.3 us
  local copies, waits for them, and re-layouts: 5.63 us -> 3.14 us
    pallas_call x1, Pallas kernels: 89.4 us -> 64.3 us  [shards(): pl.pallas_call(functools.partial(kernel, T, S), out_shape=(jax.ShapeDtype...]
    reshape x2 -> x0, local copies, waits for them, and re-layouts: 2.49 us -> none  [the longest x1 1.25 us: shards(): norm_gain.reshape(1, CH)]
where the time goes in v1:
time: 68.2 us; the launch traced here: 68.1 us
  Pallas kernels  64.3 us (94%)
  local copies, waits for them, and re-layouts  3.14 us (5%)
    pallas_call x1, Pallas kernels, shards(): pl.pallas_call(functools.partial(kernel, T, S), out_shape=(jax.ShapeDtype...  64.3 us
    unnamed x2, local copies, waits for them, and re-layouts  3.14 us

profile of v1, /device:TPU:1, one launch (start us, length us, event | category | flops | bytes accessed | tf_op | source)
XLA Modules:
  0.0 68.1 jit_solution(7991248323801348238)
XLA Ops:
  0.6 64.3 %shard_map.140 = (f32[256,128]{1,0:T(8,128)}, f32[256,128]{1,0:T(8,128)}) custom-call(s32[2]{0:T(128)} %hl_ref.1, s32[2]{0:T(128)} %ts_ref.1, f32[2]{0:T(128)} %step_ref.1, s32[16,16]{1,0:T(8,128)} %mix_ref.1, f32[320]{0:T(512)} %gain_ref.1, f32[320]{0:T(512)} %bias_ref.1, f32[128,128]{1,0:T(8,128)} %bitcast.15, f32[256,128]{1,0:T(8,128)} %bitcast.11, ...), custom_call_target="tpu_custom_call" | custom-call | tf_op jit(solution)/shard_map/pallas_call | solution.py:494
  64.9 1.6 %copy.17 = f32[2,16,8,128]{3,2,1,0:T(8,128)} copy(f32[2,16,8,128]{3,2,1,0:T(8,128)} %bitcast.13) | data formatting | bytes 262144
  66.5 1.6 %copy.18 = f32[2,16,8,128]{3,2,1,0:T(8,128)} copy(f32[2,16,8,128]{3,2,1,0:T(8,128)} %bitcast.12) | data formatting | bytes 262144

commit v2 on v1

--- a/solution.py
+++ b/solution.py
@@ -102,40 +102,41 @@
     def wait_bytes(ref, sem):
         pltpu.make_async_copy(ref, ref, sem).wait()
 
-    barrier = pltpu.get_barrier_semaphore()
-
-    def greet(tm, strip):
-        pl.semaphore_signal(
-            barrier, inc=1, device_id=(tm, strip), device_id_type=pl.DeviceIdType.MESH
-        )
-
-    for r in range(2):
-
-        @pl.when(t != rows - 2 + r)
-        def _():
-            greet(rows - 2 + r, lax.rem(s + S - 1, S))
-
-        @pl.when(t != r)
-        def _():
-            greet(r, lax.rem(s + 1, S))
-
-    def greet_column(k, _):
-        greet(lax.rem(t + k, T), s)
-        return 0
-
-    lax.fori_loop(1, T, greet_column, 0)
-
-    def greet_strips(k, _):
-        greet(t, lax.rem(s + k, S))
-        return 0
-
-    lax.fori_loop(1, S, greet_strips, 0)
     get_past = pltpu.make_async_copy(hist_hbm, hist_ref, local_sem.at[2])
     get_past.start()
     get_table = pltpu.make_async_copy(table_hbm, table, local_sem.at[0])
     get_mid = pltpu.make_async_copy(cmid_hbm, wraw, local_sem.at[1])
     get_table.start()
     get_mid.start()
+
+    barrier = pltpu.get_barrier_semaphore()
+
+    def greet(tm, strip):
+        pl.semaphore_signal(
+            barrier, inc=1, device_id=(tm, strip), device_id_type=pl.DeviceIdType.MESH
+        )
+
+    def greet_strips(k, _):
+        greet(t, lax.rem(s + k, S))
+        return 0
+
+    lax.fori_loop(1, S, greet_strips, 0)
+
+    for r in range(2):
+
+        @pl.when(t != rows - 2 + r)
+        def _():
+            greet(rows - 2 + r, lax.rem(s + S - 1, S))
+
+        @pl.when(t != r)
+        def _():
+            greet(r, lax.rem(s + 1, S))
+
+    def greet_column(k, _):
+        greet(lax.rem(t + k, T), s)
+        return 0
+
+    lax.fori_loop(1, T, greet_column, 0)
 
     for j in range(steps):
         for h in range(rows):
@@ -256,8 +257,9 @@
     wide = lax.broadcasted_iota(jnp.int32, (CHUNK, LANES), 1)
 
     def shifted(x, lanes):
-        left = jnp.where(lanes == 0, 0.0, pltpu.roll(x, 1, 1))
-        right = jnp.where(lanes == LANES - 1, 0.0, pltpu.roll(x, LANES - 1, 1))
+        zero = jnp.zeros_like(x)
+        left = jnp.where(lanes == 0, zero, pltpu.roll(x, 1, 1))
+        right = jnp.where(lanes == LANES - 1, zero, pltpu.roll(x, LANES - 1, 1))
         return left, right
 
     def first_conv(it, j):
@@ -330,11 +332,12 @@
                     x = jnp.where(s > 0, x, 0.0)
                 if r == rows + 1:
                     x = jnp.where(s < S - 1, x, 0.0)
+                x = x.astype(BF16)
                 left, right = shifted(x, wide)
                 cells = slice(r * LANES, (r + 1) * LANES)
-                hid[j, pl.ds(at, CHUNK), cells] = left.astype(BF16)
-                hid[j, pl.ds(CH + at, CHUNK), cells] = x.astype(BF16)
-                hid[j, pl.ds(2 * CH + at, CHUNK), cells] = right.astype(BF16)
+                hid[j, pl.ds(at, CHUNK), cells] = left
+                hid[j, pl.ds(CH + at, CHUNK), cells] = x
+                hid[j, pl.ds(2 * CH + at, CHUNK), cells] = right
 
         for c in range(CH // CHUNK):
             body(c)
@@ -388,40 +391,33 @@
             anchor = [
                 guess[i] - mrecv[i // steps, i % steps, 0:CIN] for i in range(total_steps)
             ]
+            odd, after, before = lax.rem(t, 2), lax.rem(s + 1, S), lax.rem(s + S - 1, S)
+            below = (t >= rows - 2) & (s < S - 1)
+            above = (t < 2) & (s > 0)
+            for k in range(T):
+                for j in range(steps * k, steps * (k + 1)):
+                    new = mixed(guess, anchor, j)
+                    sbuf[j] = new.astype(BF16)
+                    state1[j] = new
+                pair = sbuf.at[pl.ds(steps * k, steps)]
+
+                @pl.when(below)
+                def _():
+                    to(pair, xin.at[1, odd], b_send.at[1], b_recv.at[1], k, after).start()
+
+                @pl.when(above)
+                def _():
+                    to(pair, xin.at[1, rows + 2 + odd], b_send.at[2], b_recv.at[2], k, before).start()
+
+                @pl.when(t != k)
+                def _():
+                    to(pair, xin.at[1, 2 + t], b_send.at[0], b_recv.at[0], k, s).start()
+
+            xin[1, 2 + t] = sbuf[pl.ds(steps * t, steps)]
             for j in range(total_steps):
-                new = mixed(guess, anchor, j)
-                sbuf[j] = new.astype(BF16)
-                state1[j] = new
                 share = mrecv[j // steps, j % steps, 2 * CIN : 2 * CIN + 8]
                 share = jnp.concatenate([share, share], axis=0)
-                base2[j] = new + (share * guess[j] + mrecv[j // steps, j % steps, CIN : 2 * CIN])
-            xin[1, 2 + t] = sbuf[pl.ds(steps * t, steps)]
-
-            below = (t >= rows - 2) & (s < S - 1)
-            above = (t < 2) & (s > 0)
-
-            @pl.when(below)
-            def _():
-                def send_below(k, _):
-                    to(sbuf.at[pl.ds(steps * k, steps)], xin.at[1, t - (rows - 2)], b_send.at[1], b_recv.at[1], k, s + 1).start()
-                    return 0
-
-                lax.fori_loop(0, T, send_below, 0)
-
-            @pl.when(above)
-            def _():
-                def send_above(k, _):
-                    to(sbuf.at[pl.ds(steps * k, steps)], xin.at[1, rows + 2 + t], b_send.at[2], b_recv.at[2], k, s - 1).start()
-                    return 0
-
-                lax.fori_loop(0, T, send_above, 0)
-
-            def send_row(k, _):
-                other = lax.rem(t + k, T)
-                to(sbuf.at[pl.ds(steps * other, steps)], xin.at[1, 2 + t], b_send.at[0], b_recv.at[0], other, s).start()
-                return 0
-
-            lax.fori_loop(1, T, send_row, 0)
+                base2[j] = state1[j] + (share * guess[j] + mrecv[j // steps, j % steps, CIN : 2 * CIN])
             wait_bytes(sbuf.at[pl.ds(0, steps * (T - 1))], b_send.at[0])
 
             @pl.when(below)
@@ -445,17 +441,16 @@
         else:
             guess = row_guess(it)
             anchor = [guess[i] - base2[i] for i in range(total_steps)]
-            for j in range(total_steps):
-                osend[j, 1] = guess[j] - state1[j]
-                osend[j, 0] = mixed(guess, anchor, j)
+            for k in range(T):
+                for j in range(steps * k, steps * (k + 1)):
+                    osend[j, 1] = guess[j] - state1[j]
+                    osend[j, 0] = mixed(guess, anchor, j)
+
+                @pl.when(t != k)
+                def _():
+                    to(osend.at[pl.ds(steps * k, steps)], orecv.at[t], o_send, o_recv, k, s).start()
+
             orecv[t] = osend[pl.ds(steps * t, steps)]
-
-            def send_out(k, _):
-                other = lax.rem(t + k, T)
-                to(osend.at[pl.ds(steps * other, steps)], orecv.at[t], o_send, o_recv, other, s).start()
-                return 0
-
-            lax.fori_loop(1, T, send_out, 0)
             wait_bytes(orecv.at[pl.ds(0, T - 1)], o_send)
             wait_bytes(orecv.at[pl.ds(0, T - 1)], o_recv)
             for j in range(steps):
@@ -554,9 +549,10 @@
             conv_mid,
             history.reshape(history.shape[0] * flat, width),
         )
+        valid = history_length[0] > 0
         return (
-            iterate.reshape(trajectory.shape),
-            residual.reshape(trajectory.shape),
+            jnp.where(valid, iterate, residual).reshape(trajectory.shape),
+            jnp.where(valid, residual, iterate).reshape(trajectory.shape),
         )
 
     return jax.shard_map(

time: 68.2 us -> 65.5 us (0.960)
  local copies, waits for them, and re-layouts: 3.14 us -> 0 us
  Pallas kernels: 64.3 us -> 62.4 us
  other arithmetic: 0 us -> 1.69 us
    unnamed x2 -> x0, local copies, waits for them, and re-layouts: 3.14 us -> none
    pallas_call x1, Pallas kernels: 64.3 us -> 62.4 us  [shards(): pl.pallas_call(functools.partial(kernel, T, S), out_shape=(jax.ShapeDtype...]
    select_n x0 -> x1, other arithmetic: none -> 1.69 us  [shards(): jnp.where(valid, residual, iterate).reshape(trajectory.shape)]
where the time goes in v2:
time: 65.5 us; the launch traced here: 65.4 us
  Pallas kernels  62.4 us (95%)
  other arithmetic  1.69 us (3%)
  between operations  1.29 us (2%)
    pallas_call x1, Pallas kernels, shards(): pl.pallas_call(functools.partial(kernel, T, S), out_shape=(jax.ShapeDtype...  62.4 us
    select_n x1, other arithmetic, shards(): jnp.where(valid, residual, iterate).reshape(trajectory.shape)  1.69 us

profile of v2, /device:TPU:1, one launch (start us, length us, event | category | flops | bytes accessed | tf_op | source)
XLA Modules:
  0.0 65.4 jit_solution(4559770599268481441)
XLA Ops:
  1.3 62.4 %shard_map.140 = (f32[256,128]{1,0:T(8,128)}, f32[256,128]{1,0:T(8,128)}) custom-call(s32[2]{0:T(128)} %hl_ref.1, s32[2]{0:T(128)} %ts_ref.1, f32[2]{0:T(128)} %step_ref.1, s32[16,16]{1,0:T(8,128)} %mix_ref.1, f32[320]{0:T(512)} %gain_ref.1, f32[320]{0:T(512)} %bias_ref.1, f32[128,128]{1,0:T(8,128)} %bitcast.17, f32[256,128]{1,0:T(8,128)} %bitcast.13, ...), custom_call_target="tpu_custom_call" | custom-call | tf_op jit(solution)/shard_map/pallas_call | solution.py:489
  63.7 1.7 %broadcast_select_fusion = (f32[256,128]{1,0:T(8,128)}, f32[256,128]{1,0:T(8,128)}) fusion(f32[256,128]{1,0:T(8,128)} %get-tuple-element.5, f32[256,128]{1,0:T(8,128)} %get-tuple-element.4, pred[]{:T(512)} %bitcast), kind=kLoop, calls=%fused_computation | loop fusion | flops 65536 | bytes 524289 | tf_op jit(solution)/shard_map/jit(_where)/select_n | solution.py:555

commit v3 on v2

--- a/solution.py
+++ b/solution.py
@@ -9,7 +9,6 @@
 
 F32 = jnp.float32
 BF16 = jnp.bfloat16
-HIGHEST = lax.Precision.HIGHEST
 GROUPS = 32
 ITERS = 2
 EPSILON = 1e-05
@@ -21,6 +20,13 @@
 def silu(v):
     half = 0.5 * v
     return half + half * jnp.tanh(half)
+
+
+def thirds(x):
+    high = x.astype(BF16)
+    rest = x - high.astype(F32)
+    middle = rest.astype(BF16)
+    return high, middle, (rest - middle.astype(F32)).astype(BF16)
 
 
 def kernel(
@@ -293,11 +299,18 @@
 
         for c in range(CH // CHUNK):
             add_up(c)
-        by_channel = lax.dot_general(
-            jnp.ones((8, LANES), F32), sums[...], (((1,), (1,)), ((), ())), precision=HIGHEST,
-            preferred_element_type=F32,
-        )
-        by_group = jnp.dot(by_channel, ind[...], precision=HIGHEST, preferred_element_type=F32)
+        ones = jnp.ones((8, LANES), BF16)
+        by_channel = None
+        for part in thirds(sums[...]):
+            product = lax.dot_general(
+                ones, part, (((1,), (1,)), ((), ())), preferred_element_type=F32
+            )
+            by_channel = product if by_channel is None else by_channel + product
+        which = ind[...].astype(BF16)
+        by_group = None
+        for part in thirds(by_channel):
+            product = jnp.dot(part, which, preferred_element_type=F32)
+            by_group = product if by_group is None else by_group + product
         stat[k] = by_group[0:1]
         stats[k, s] = by_group[0:1]
 
@@ -488,7 +501,7 @@
         dma = pltpu.SemaphoreType.DMA
         iterate, residual = pl.pallas_call(
             functools.partial(kernel, T, S),
-            out_shape=(jax.ShapeDtypeStruct((flat, width), F32),) * 2,
+            out_shape=(pltpu.VMEM((flat, width), F32),) * 2,
             in_specs=[smem] * 4 + [vmem] * 6 + [hbm] * 3,
             out_specs=(vmem, vmem),
             scratch_shapes=[

time: 65.5 us -> 63.8 us (0.974)
  other arithmetic: 1.69 us -> 0.72 us
  Pallas kernels: 62.4 us -> 61.7 us
    select_n x1, other arithmetic: 1.69 us -> 0.72 us  [shards(): jnp.where(valid, residual, iterate).reshape(trajectory.shape)]
    pallas_call x1, Pallas kernels: 62.4 us -> 61.7 us  [shards(): pl.pallas_call(functools.partial(kernel, T, S), out_shape=(pltpu.VMEM((fl...]
where the time goes in v3:
time: 63.8 us; the launch traced here: 63.7 us
  Pallas kernels  61.7 us (97%)
  between operations  1.29 us (2%)
  other arithmetic  0.72 us (1%)
    pallas_call x1, Pallas kernels, shards(): pl.pallas_call(functools.partial(kernel, T, S), out_shape=(pltpu.VMEM((fl...  61.7 us

profile of v3, /device:TPU:1, one launch (start us, length us, event | category | flops | bytes accessed | tf_op | source)
XLA Modules:
  0.0 63.7 jit_solution(13628795218162353310)
XLA Ops:
  1.3 61.7 %shard_map.140 = (f32[256,128]{1,0:T(8,128)S(1)}, f32[256,128]{1,0:T(8,128)S(1)}) custom-call(s32[2]{0:T(128)} %hl_ref.1, s32[2]{0:T(128)} %ts_ref.1, f32[2]{0:T(128)} %step_ref.1, s32[16,16]{1,0:T(8,128)} %mix_ref.1, f32[320]{0:T(512)} %gain_ref.1, f32[320]{0:T(512)} %bias_ref.1, f32[128,128]{1,0:T(8,128)} %bitcast.17, f32[256,128]{1,0:T(8,128)} %bitcast.13, ...), custom_call_target="tpu_custom_call" | custom-call | tf_op jit(solution)/shard_map/pallas_call | solution.py:502
  62.9 0.7 %broadcast_select_fusion = (f32[256,128]{1,0:T(8,128)}, f32[256,128]{1,0:T(8,128)}) fusion(f32[256,128]{1,0:T(8,128)S(1)} %get-tuple-element.5, f32[256,128]{1,0:T(8,128)S(1)} %get-tuple-element.4, pred[]{:T(512)} %bitcast), kind=kLoop, calls=%fused_computation | loop fusion | flops 65536 | bytes 524289 | tf_op jit(solution)/shard_map/jit(_where)/select_n | solution.py:568

commit v4 on v3

--- a/solution.py
+++ b/solution.py
@@ -243,22 +243,6 @@
             ).astype(BF16)
             before = turned_by[k]
 
-    @pl.when(s < S - 1)
-    def _():
-        send_down.wait_send()
-
-    @pl.when(s > 0)
-    def _():
-        send_up.wait_send()
-
-    @pl.when(s > 0)
-    def _():
-        send_down.wait_recv()
-
-    @pl.when(s < S - 1)
-    def _():
-        send_up.wait_recv()
-
     lane = lax.broadcasted_iota(jnp.int32, (CIN, LANES), 1)
     wide = lax.broadcasted_iota(jnp.int32, (CHUNK, LANES), 1)
 
@@ -268,20 +252,45 @@
         right = jnp.where(lanes == LANES - 1, zero, pltpu.roll(x, LANES - 1, 1))
         return left, right
 
-    def first_conv(it, j):
-        for r in range(rows + 4):
+    def first_conv(it, j, rows_in, rows_out):
+        for r in rows_in:
             block = xin[it, r, j]
             left, right = shifted(block.astype(F32), lane)
-            xs[0:CIN, r * LANES : (r + 1) * LANES] = left.astype(BF16)
-            xs[CIN : 2 * CIN, r * LANES : (r + 1) * LANES] = block
-            xs[2 * CIN : 3 * CIN, r * LANES : (r + 1) * LANES] = right.astype(BF16)
-        for r in range(0, rows + 2, 2):
+            xs[j, 0:CIN, r * LANES : (r + 1) * LANES] = left.astype(BF16)
+            xs[j, CIN : 2 * CIN, r * LANES : (r + 1) * LANES] = block
+            xs[j, 2 * CIN : 3 * CIN, r * LANES : (r + 1) * LANES] = right.astype(BF16)
+        for r in rows_out:
             taps = jnp.concatenate(
-                [xs[:, (r + a) * LANES : (r + a + 2) * LANES] for a in range(3)], axis=0
+                [xs[j, :, (r + a) * LANES : (r + a + 2) * LANES] for a in range(3)], axis=0
             )
             early[j, :, r * LANES : (r + 2) * LANES] = (
                 jnp.dot(win[...], taps, preferred_element_type=F32) + embcol[j]
             )
+
+    def inner_rows(it):
+        for j in range(steps):
+            first_conv(it, j, range(2, rows + 2), range(2, rows, 2))
+
+    def outer_rows(it, j):
+        first_conv(it, j, (0, 1, rows + 2, rows + 3), (0, rows))
+
+    inner_rows(0)
+
+    @pl.when(s < S - 1)
+    def _():
+        send_down.wait_send()
+
+    @pl.when(s > 0)
+    def _():
+        send_up.wait_send()
+
+    @pl.when(s > 0)
+    def _():
+        send_down.wait_recv()
+
+    @pl.when(s < S - 1)
+    def _():
+        send_up.wait_recv()
 
     def send_sums(it, j):
         k = it * steps + j
@@ -392,7 +401,7 @@
 
     for it in range(ITERS):
         for j in range(steps):
-            first_conv(it, j)
+            outer_rows(it, j)
             send_sums(it, j)
         for j in range(steps):
             normalise(it, j)
@@ -442,6 +451,7 @@
                 wait_bytes(sbuf, b_send.at[2])
 
             wait_bytes(sbuf.at[pl.ds(0, steps * (T - 1))], b_recv.at[0])
+            inner_rows(1)
 
             @pl.when(s > 0)
             def _():
@@ -511,7 +521,7 @@
                 pltpu.VMEM((3, CH, 3 * CH), BF16),
                 pltpu.VMEM((CH, 9 * CIN), BF16),
                 pltpu.VMEM((ITERS, rows + 4, steps, CIN, width), BF16),
-                pltpu.VMEM((3 * CIN, (rows + 4) * width), BF16),
+                pltpu.VMEM((steps, 3 * CIN, (rows + 4) * width), BF16),
                 pltpu.VMEM((steps, CH, (rows + 2) * width), F32),
                 pltpu.VMEM((steps, 3 * CH, (rows + 2) * width), BF16),
                 pltpu.VMEM((CH, 1), F32),

time: 63.8 us -> 63.3 us (level)
  no operation moved by 1% of the time
where the time goes in v4:
time: 63.3 us; the launch traced here: 63.2 us
  Pallas kernels  61.2 us (97%)
  between operations  1.29 us (2%)
  other arithmetic  0.72 us (1%)
    pallas_call x1, Pallas kernels, shards(): pl.pallas_call(functools.partial(kernel, T, S), out_shape=(pltpu.VMEM((fl...  61.2 us

profile of v4, /device:TPU:1, one launch (start us, length us, event | category | flops | bytes accessed | tf_op | source)
XLA Modules:
  0.0 63.2 jit_solution(3988388975444647878)
XLA Ops:
  1.3 61.2 %shard_map.140 = (f32[256,128]{1,0:T(8,128)S(1)}, f32[256,128]{1,0:T(8,128)S(1)}) custom-call(s32[2]{0:T(128)} %hl_ref.1, s32[2]{0:T(128)} %ts_ref.1, f32[2]{0:T(128)} %step_ref.1, s32[16,16]{1,0:T(8,128)} %mix_ref.1, f32[320]{0:T(512)} %gain_ref.1, f32[320]{0:T(512)} %bias_ref.1, f32[128,128]{1,0:T(8,128)} %bitcast.17, f32[256,128]{1,0:T(8,128)} %bitcast.13, ...), custom_call_target="tpu_custom_call" | custom-call | tf_op jit(solution)/shard_map/pallas_call | solution.py:512
  62.5 0.7 %broadcast_select_fusion = (f32[256,128]{1,0:T(8,128)}, f32[256,128]{1,0:T(8,128)}) fusion(f32[256,128]{1,0:T(8,128)S(1)} %get-tuple-element.5, f32[256,128]{1,0:T(8,128)S(1)} %get-tuple-element.4, pred[]{:T(512)} %bitcast), kind=kLoop, calls=%fused_computation | loop fusion | flops 65536 | bytes 524289 | tf_op jit(solution)/shard_map/jit(_where)/select_n | solution.py:578

commit v5 on v4

--- a/solution.py
+++ b/solution.py
@@ -267,9 +267,22 @@
                 jnp.dot(win[...], taps, preferred_element_type=F32) + embcol[j]
             )
 
+    def add_up(j, rows_in, fresh):
+        for at in range(0, CH, CHUNK):
+            total = square = jnp.zeros((CHUNK, LANES), F32)
+            if not fresh:
+                total, square = sums[j, pl.ds(at, CHUNK)], sums[j, pl.ds(CH + at, CHUNK)]
+            for r in rows_in:
+                x = early[j, pl.ds(at, CHUNK), r * LANES : (r + 1) * LANES]
+                total += x
+                square += x * x
+            sums[j, pl.ds(at, CHUNK)] = total
+            sums[j, pl.ds(CH + at, CHUNK)] = square
+
     def inner_rows(it):
         for j in range(steps):
             first_conv(it, j, range(2, rows + 2), range(2, rows, 2))
+            add_up(j, range(2, rows), True)
 
     def outer_rows(it, j):
         first_conv(it, j, (0, 1, rows + 2, rows + 3), (0, rows))
@@ -295,22 +308,10 @@
     def send_sums(it, j):
         k = it * steps + j
 
-        def add_up(c):
-            at = c * CHUNK
-            total = jnp.zeros((CHUNK, LANES), F32)
-            square = jnp.zeros((CHUNK, LANES), F32)
-            for r in range(1, rows + 1):
-                x = early[j, pl.ds(at, CHUNK), r * LANES : (r + 1) * LANES]
-                total += x
-                square += x * x
-            sums[pl.ds(at, CHUNK)] = total
-            sums[pl.ds(CH + at, CHUNK)] = square
-
-        for c in range(CH // CHUNK):
-            add_up(c)
+        add_up(j, (1, rows), False)
         ones = jnp.ones((8, LANES), BF16)
         by_channel = None
-        for part in thirds(sums[...]):
+        for part in thirds(sums[j]):
             product = lax.dot_general(
                 ones, part, (((1,), (1,)), ((), ())), preferred_element_type=F32
             )
@@ -528,7 +529,7 @@
                 pltpu.VMEM((CH, 1), F32),
                 pltpu.VMEM((steps, CH, 1), F32),
                 pltpu.VMEM((2 * CH, width), F32),
-                pltpu.VMEM((2 * CH, width), F32),
+                pltpu.VMEM((steps, 2 * CH, width), F32),
                 pltpu.VMEM((ITERS * steps, 1, width), F32),
                 pltpu.VMEM((ITERS * steps, S, 1, width), F32),
                 pltpu.VMEM((ITERS, rows, steps, CIN, width), F32),

time: 63.3 us -> 63.2 us (level)
  no operation moved by 1% of the time
where the time goes in v5:
time: 63.2 us; the launch traced here: 63.1 us
  Pallas kernels  61.1 us (97%)
  between operations  1.29 us (2%)
  other arithmetic  0.72 us (1%)
    pallas_call x1, Pallas kernels, shards(): pl.pallas_call(functools.partial(kernel, T, S), out_shape=(pltpu.VMEM((fl...  61.1 us

profile of v5, /device:TPU:1, one launch (start us, length us, event | category | flops | bytes accessed | tf_op | source)
XLA Modules:
  0.0 63.1 jit_solution(10145256799400827592)
XLA Ops:
  1.3 61.1 %shard_map.140 = (f32[256,128]{1,0:T(8,128)S(1)}, f32[256,128]{1,0:T(8,128)S(1)}) custom-call(s32[2]{0:T(128)} %hl_ref.1, s32[2]{0:T(128)} %ts_ref.1, f32[2]{0:T(128)} %step_ref.1, s32[16,16]{1,0:T(8,128)} %mix_ref.1, f32[320]{0:T(512)} %gain_ref.1, f32[320]{0:T(512)} %bias_ref.1, f32[128,128]{1,0:T(8,128)} %bitcast.17, f32[256,128]{1,0:T(8,128)} %bitcast.13, ...), custom_call_target="tpu_custom_call" | custom-call | tf_op jit(solution)/shard_map/pallas_call | solution.py:513
  62.4 0.7 %broadcast_select_fusion = (f32[256,128]{1,0:T(8,128)}, f32[256,128]{1,0:T(8,128)}) fusion(f32[256,128]{1,0:T(8,128)S(1)} %get-tuple-element.5, f32[256,128]{1,0:T(8,128)S(1)} %get-tuple-element.4, pred[]{:T(512)} %bitcast), kind=kLoop, calls=%fused_computation | loop fusion | flops 65536 | bytes 524289 | tf_op jit(solution)/shard_map/jit(_where)/select_n | solution.py:579
